TPU v7x, 32 devices: a whole 2x2x4 slice. The times are simulated.
32 devices in a mesh: rep: 4 (over y, x), shard: 8 (over z, core).
Axes of the slice: x: 2, y: 2, z: 4, core: 2. Of those that a mesh axis runs over, the one named last changes fastest.
Arguments:
- tokens: bfloat16 [16, 2048, 768], P('shard', 'rep'), may hold values from -6 to 6
- segment_ids: int32 [16, 2048], P('shard'), may hold values from 0 to 7, never falling along the last dimension, each value on 1 to 1024 neighbouring positions
- cotangent: bfloat16 [16, 2048, 768], P('shard', 'rep'), may hold values from -6 to 6
- query_weight: bfloat16 [768, 768], P('shard'), may hold values from -0.3125 to 0.3125
- key_weight: bfloat16 [768, 768], P('shard'), may hold values from -0.3125 to 0.3125
- value_weight: bfloat16 [768, 768], P('shard'), may hold values from -0.21875 to 0.21875
- output_weight: bfloat16 [768, 768], P('shard'), may hold values from -1.5 to 1.5
- expand_weight: bfloat16 [768, 3072], P('shard'), may hold values from -0.21875 to 0.21875
- reduce_weight: bfloat16 [3072, 768], P('shard'), may hold values from -0.109375 to 0.109375
- query_bias: bfloat16 [768], P('shard'), may hold values from -1.5 to 1.5
- value_bias: bfloat16 [768], P('shard'), may hold values from -0.5 to 0.5
- output_bias: bfloat16 [768], P('shard'), may hold values from -1.5 to 1.5
- expand_bias: bfloat16 [3072], P('shard'), may hold values from -1.5 to 1.5
- reduce_bias: bfloat16 [768], P('shard'), may hold values from -1.5 to 1.5
- first_gain: bfloat16 [768], P('shard'), may hold values from 0.099609375 to 1.8984375
- first_shift: bfloat16 [768], P('shard'), may hold values from -1.5 to 1.5
- second_gain: bfloat16 [768], P('shard'), may hold values from 0.099609375 to 1.8984375
- second_shift: bfloat16 [768], P('shard'), may hold values from -1.5 to 1.5
Outputs:
- layer_output: bfloat16 [16, 2048, 768], P('shard', 'rep')
- tokens_gradient: bfloat16 [16, 2048, 768], P('shard', 'rep')
- query_weight_gradient: float32 [768, 768], P('shard')
- key_weight_gradient: float32 [768, 768], P('shard')
- value_weight_gradient: float32 [768, 768], P('shard')
- output_weight_gradient: float32 [768, 768], P('shard')
- expand_weight_gradient: float32 [768, 3072], P('shard')
- reduce_weight_gradient: float32 [3072, 768], P('shard')
- query_bias_gradient: float32 [768], P('shard')
- value_bias_gradient: float32 [768], P('shard')
- output_bias_gradient: float32 [768], P('shard')
- expand_bias_gradient: float32 [3072], P('shard')
- reduce_bias_gradient: float32 [768], P('shard')
- first_gain_gradient: float32 [768], P('shard')
- first_shift_gradient: float32 [768], P('shard')
- second_gain_gradient: float32 [768], P('shard')
- second_shift_gradient: float32 [768], P('shard')
Inputs may be any that keep to these rules, and one draw needn't show every extreme that they name: `segment_ids`: within each sequence the ids never fall; each document holds 1 to 1024 positions and some document of each sequence exactly 1024.
All inputs are finite; a program needn't handle non-finite values.
Results may differ from a plain program's by a relative error of at most 0.017.
The roundings to bfloat16 on the way count: a program that leaves them out, or rounds other values in their place, can miss the bound.
Values may be sent and summed in bfloat16 or wider, within the bound.
A program may use at most 448 MiB of HBM per device.

v0:
```python
from functools import partial
import jax
import jax.numpy as jnp
from jax import lax
from jax.sharding import PartitionSpec as P

HEAD_DIM = 64
masked_value = -1e30
norm_eps = 1e-05


def as_sent(array):
    return jax.tree.map(lambda a: a.astype(jnp.bfloat16) if a.dtype == jnp.float32 else a, array)


def norm_rows(values, gain, shift):
    centre = values - jnp.mean(values, axis=-1, keepdims=True)
    spread = jnp.mean(centre * centre, axis=-1, keepdims=True)
    return centre * lax.rsqrt(spread + norm_eps) * gain + shift


def dense(left, right):
    return jnp.dot(left, right, preferred_element_type=jnp.float32)


def dense_left(left, right):
    return lax.dot_general(
        left, right, (((0,), (0,)), ((), ())), preferred_element_type=jnp.float32
    )


def dense_right(left, right):
    return lax.dot_general(
        left, right, (((1,), (1,)), ((), ())), preferred_element_type=jnp.float32
    )


def column_sum(values):
    return jnp.sum(values.astype(jnp.float32), axis=0)


def unpack(weights):
    matrices = weights[:6]
    vectors = tuple((member.astype(jnp.float32) for member in weights[6:]))
    return (matrices, vectors)


def block_scores(query_block, key_heads, allowed_blocks, block_rows):
    factor = query_block.shape[2] ** (-0.5)
    pieces = []
    for number in range(len(allowed_blocks)):
        allowed = allowed_blocks[number]
        key_block = key_heads[number * block_rows : (number + 1) * block_rows]
        product = partial(
            jnp.einsum, "qhd,khd->hqk", query_block, key_block, preferred_element_type=jnp.float32
        )
        unmasked = product()
        pieces.append(jnp.where(allowed[None, :, :], unmasked * factor, masked_value))
    return jnp.concatenate(pieces, axis=2)


def allowed_for(query_segments, segment_keys, block_rows, key_count):
    return [
        query_segments[:, None]
        == segment_keys[number * block_rows : (number + 1) * block_rows][None, :]
        for number in range(key_count)
    ]


def attend_forward(query_heads, key_heads, value_heads, segment_query, segment_whole):
    local_rows = query_heads.shape[0]
    block_rows = min(512, local_rows)
    key_count = key_heads.shape[0] // block_rows
    allowed_blocks = allowed_for(segment_query, segment_whole, block_rows, key_count)
    scores = block_scores(query_heads, key_heads, allowed_blocks, block_rows)
    largest = jnp.max(scores, axis=2, keepdims=True)
    exponent = jnp.exp(scores - largest)
    row_total = jnp.sum(exponent, axis=2, keepdims=True)
    chances = (exponent / row_total).astype(jnp.bfloat16)
    logsums = [largest[:, :, 0] + jnp.log(row_total[:, :, 0])]
    mixture = jnp.zeros(query_heads.shape, jnp.float32)
    for number in range(key_count):
        chance_slice = chances[:, :, number * block_rows : (number + 1) * block_rows]
        value_block = value_heads[number * block_rows : (number + 1) * block_rows]
        product = partial(
            jnp.einsum,
            "hqk,khd->qhd",
            chance_slice,
            value_block,
            preferred_element_type=jnp.float32,
        )
        mixture = mixture + product()
    mixtures = [mixture]
    return (jnp.concatenate(mixtures, axis=0), jnp.concatenate(logsums, axis=1))


def attend_backward(
    query_heads,
    key_heads,
    value_heads,
    segment_query,
    segment_keys,
    logsums,
    grad_heads,
    block_rows,
):
    query_rows, head_count, head_width = query_heads.shape
    key_count = key_heads.shape[0] // block_rows
    factor = head_width ** (-0.5)
    block_shape = (block_rows, head_count, head_width)
    key_grads = [jnp.zeros(block_shape, jnp.float32) for number in range(key_count)]
    value_grads = [jnp.zeros(block_shape, jnp.float32) for number in range(key_count)]
    allowed_blocks = allowed_for(segment_query, segment_keys, block_rows, key_count)
    scores = block_scores(query_heads, key_heads, allowed_blocks, block_rows)
    chances = jnp.exp(scores - logsums[:, 0:block_rows, None])
    chance_low = chances.astype(jnp.bfloat16)
    pieces = []
    for number in range(key_count):
        value_block = value_heads[number * block_rows : (number + 1) * block_rows]
        product = partial(
            jnp.einsum, "qhd,khd->hqk", grad_heads, value_block, preferred_element_type=jnp.float32
        )
        pieces.append(product())
    grad_chances = jnp.concatenate(pieces, axis=2)
    centre = jnp.sum(chances * grad_chances, axis=2, keepdims=True)
    centres = [centre[:, :, 0]]
    grad_scores = (chances * (grad_chances - centre)).astype(jnp.bfloat16)
    query_grad = jnp.zeros(block_shape, jnp.float32)
    for number in range(key_count):
        key_block = key_heads[number * block_rows : (number + 1) * block_rows]
        score_slice = grad_scores[:, :, number * block_rows : (number + 1) * block_rows]
        chance_slice = chance_low[:, :, number * block_rows : (number + 1) * block_rows]
        query_grad = (
            query_grad
            + partial(
                jnp.einsum,
                "hqk,khd->qhd",
                score_slice,
                key_block,
                preferred_element_type=jnp.float32,
            )()
        )
        key_grads[number] = (
            key_grads[number]
            + partial(
                jnp.einsum,
                "hqk,qhd->khd",
                score_slice,
                query_heads,
                preferred_element_type=jnp.float32,
            )()
        )
        value_grads[number] = (
            value_grads[number]
            + partial(
                jnp.einsum,
                "hqk,qhd->khd",
                chance_slice,
                grad_heads,
                preferred_element_type=jnp.float32,
            )()
        )
    query_grads = [query_grad * factor]
    key_whole = jnp.concatenate(key_grads, axis=0) * factor
    return (
        jnp.concatenate(query_grads, axis=0),
        key_whole,
        jnp.concatenate(value_grads, axis=0),
        jnp.concatenate(centres, axis=1),
    )


def local(
    tokens,
    segment_ids,
    cotangent,
    query_weight,
    key_weight,
    value_weight,
    output_weight,
    expand_weight,
    reduce_weight,
    query_bias,
    value_bias,
    output_bias,
    expand_bias,
    reduce_bias,
    first_gain,
    first_shift,
    second_gain,
    second_shift,
):
    shards = (
        query_weight,
        key_weight,
        value_weight,
        output_weight,
        expand_weight,
        reduce_weight,
        query_bias,
        value_bias,
        output_bias,
        expand_bias,
        reduce_bias,
        first_gain,
        first_shift,
        second_gain,
        second_shift,
    )
    micro_count = tokens.shape[0]
    local_rows = tokens.shape[1]
    model_width = tokens.shape[2]
    head_count = model_width // HEAD_DIM
    block_rows = min(512, local_rows)
    offset = lax.axis_index("rep") * local_rows
    totals = tuple(
        (
            jnp.zeros((lax.axis_size("shard") * member.shape[0],) + member.shape[1:], jnp.float32)
            for member in shards
        )
    )
    outputs = []
    input_grads = []

    def heads_of(array):
        return array.reshape(array.shape[0], head_count, HEAD_DIM)

    for micro_index in range(micro_count):
        weights_now = (
            lax.all_gather(shards[0], "shard", axis=0, tiled=True),
            lax.all_gather(shards[1], "shard", axis=0, tiled=True),
            lax.all_gather(shards[2], "shard", axis=0, tiled=True),
            lax.all_gather(shards[3], "shard", axis=0, tiled=True),
            lax.all_gather(shards[4], "shard", axis=0, tiled=True),
            lax.all_gather(shards[5], "shard", axis=0, tiled=True),
            lax.all_gather(shards[6], "shard", axis=0, tiled=True),
            lax.all_gather(shards[7], "shard", axis=0, tiled=True),
            lax.all_gather(shards[8], "shard", axis=0, tiled=True),
            lax.all_gather(shards[9], "shard", axis=0, tiled=True),
            lax.all_gather(shards[10], "shard", axis=0, tiled=True),
            lax.all_gather(shards[11], "shard", axis=0, tiled=True),
            lax.all_gather(shards[12], "shard", axis=0, tiled=True),
            lax.all_gather(shards[13], "shard", axis=0, tiled=True),
            lax.all_gather(shards[14], "shard", axis=0, tiled=True),
        )
        matrices, vectors = unpack(weights_now)
        query_matrix, key_matrix, value_matrix, output_matrix, expand_matrix, reduce_matrix = (
            matrices
        )
        (
            query_vector,
            value_vector,
            output_vector,
            expand_vector,
            reduce_vector,
            first_gain_vec,
            first_shift_vec,
            second_gain_vec,
            second_shift_vec,
        ) = vectors
        inputs_now = tokens[micro_index]
        segment_whole = segment_ids[micro_index]
        segment_query = lax.dynamic_slice_in_dim(segment_whole, offset, local_rows)
        queries = (dense(inputs_now, query_matrix) + query_vector).astype(jnp.bfloat16)
        keys_local = dense(inputs_now, key_matrix).astype(jnp.bfloat16)
        values_local = (dense(inputs_now, value_matrix) + value_vector).astype(jnp.bfloat16)
        keys_whole, values_whole = (
            lax.all_gather(keys_local, "rep", axis=0, tiled=True),
            lax.all_gather(values_local, "rep", axis=0, tiled=True),
        )
        mixture, logsums = attend_forward(
            heads_of(queries),
            heads_of(keys_whole),
            heads_of(values_whole),
            segment_query,
            segment_whole,
        )
        attended = mixture.reshape(local_rows, model_width).astype(jnp.bfloat16)
        branch = dense(attended, output_matrix) + output_vector
        first, first_back = jax.vjp(
            norm_rows, inputs_now.astype(jnp.float32) + branch, first_gain_vec, first_shift_vec
        )
        first_low = first.astype(jnp.bfloat16)
        expanded = dense(first_low, expand_matrix) + expand_vector
        activated, gelu_back = jax.vjp(jax.nn.gelu, expanded)
        activated_low = activated.astype(jnp.bfloat16)
        reduced = dense(activated_low, reduce_matrix) + reduce_vector
        result, second_back = jax.vjp(norm_rows, first + reduced, second_gain_vec, second_shift_vec)
        outputs.append(result.astype(jnp.bfloat16))
        weights_now = (
            lax.all_gather(shards[0], "shard", axis=0, tiled=True),
            lax.all_gather(shards[1], "shard", axis=0, tiled=True),
            lax.all_gather(shards[2], "shard", axis=0, tiled=True),
            lax.all_gather(shards[3], "shard", axis=0, tiled=True),
            lax.all_gather(shards[4], "shard", axis=0, tiled=True),
            lax.all_gather(shards[5], "shard", axis=0, tiled=True),
            lax.all_gather(shards[6], "shard", axis=0, tiled=True),
            lax.all_gather(shards[7], "shard", axis=0, tiled=True),
            lax.all_gather(shards[8], "shard", axis=0, tiled=True),
            lax.all_gather(shards[9], "shard", axis=0, tiled=True),
            lax.all_gather(shards[10], "shard", axis=0, tiled=True),
            lax.all_gather(shards[11], "shard", axis=0, tiled=True),
            lax.all_gather(shards[12], "shard", axis=0, tiled=True),
            lax.all_gather(shards[13], "shard", axis=0, tiled=True),
            lax.all_gather(shards[14], "shard", axis=0, tiled=True),
        )
        matrices, vectors = unpack(weights_now)
        query_matrix, key_matrix, value_matrix, output_matrix, expand_matrix, reduce_matrix = (
            matrices
        )
        grad_second, grad_second_gain, grad_second_shift = second_back(
            cotangent[micro_index].astype(jnp.float32)
        )
        grad_reduced = grad_second.astype(jnp.bfloat16)
        reduce_matrix_grad = dense_left(activated_low, grad_reduced)
        (grad_expanded_full,) = gelu_back(dense_right(grad_reduced, reduce_matrix))
        grad_expanded = grad_expanded_full.astype(jnp.bfloat16)
        expand_matrix_grad = dense_left(first_low, grad_expanded)
        grad_first = grad_second + dense_right(grad_expanded, expand_matrix)
        grad_residual, grad_first_gain, grad_first_shift = first_back(grad_first)
        grad_branch = grad_residual.astype(jnp.bfloat16)
        output_matrix_grad = dense_left(attended, grad_branch)
        grad_attended = dense_right(grad_branch, output_matrix).astype(jnp.bfloat16)
        query_side = attend_backward(
            heads_of(queries),
            heads_of(keys_whole),
            heads_of(values_whole),
            segment_query,
            segment_whole,
            logsums,
            heads_of(grad_attended),
            block_rows,
        )
        grad_query_heads = query_side[0]
        key_terms = query_side[1]
        value_terms = query_side[2]
        sequence_rows = key_terms.shape[0]
        grad_keys_full, grad_values_full = (
            lax.psum_scatter(
                key_terms.reshape(sequence_rows, model_width),
                "rep",
                scatter_dimension=0,
                tiled=True,
            ),
            lax.psum_scatter(
                value_terms.reshape(sequence_rows, model_width),
                "rep",
                scatter_dimension=0,
                tiled=True,
            ),
        )
        grad_queries = grad_query_heads.reshape(local_rows, model_width).astype(jnp.bfloat16)
        grad_keys = grad_keys_full.astype(jnp.bfloat16)
        grad_values = grad_values_full.astype(jnp.bfloat16)
        grad_inputs = (
            grad_residual
            + dense_right(grad_queries, query_matrix)
            + dense_right(grad_keys, key_matrix)
            + dense_right(grad_values, value_matrix)
        )
        input_grads.append(grad_inputs.astype(jnp.bfloat16))
        changes = (
            dense_left(inputs_now, grad_queries),
            dense_left(inputs_now, grad_keys),
            dense_left(inputs_now, grad_values),
            output_matrix_grad,
            expand_matrix_grad,
            reduce_matrix_grad,
            column_sum(grad_queries),
            column_sum(grad_values),
            column_sum(grad_branch),
            column_sum(grad_expanded),
            column_sum(grad_reduced),
            grad_first_gain,
            grad_first_shift,
            grad_second_gain,
            grad_second_shift,
        )
        totals = tuple((total + change for total, change in zip(totals, changes)))
    summed = lax.psum_scatter(totals, "shard", scatter_dimension=0, tiled=True)
    final = jax.tree.map(lambda part: part.astype(jnp.float32), lax.psum(as_sent(summed), "rep"))
    return (jnp.stack(outputs), jnp.stack(input_grads)) + tuple(final)


def solution(mesh):
    in_specs = (
        P("shard", "rep", None),
        P("shard", None),
        P("shard", "rep", None),
        P("shard", None),
        P("shard", None),
        P("shard", None),
        P("shard", None),
        P("shard", None),
        P("shard", None),
        P("shard"),
        P("shard"),
        P("shard"),
        P("shard"),
        P("shard"),
        P("shard"),
        P("shard"),
        P("shard"),
        P("shard"),
    )
    out_specs = (
        P("shard", "rep", None),
        P("shard", "rep", None),
        P("shard", None),
        P("shard", None),
        P("shard", None),
        P("shard", None),
        P("shard", None),
        P("shard", None),
        P("shard"),
        P("shard"),
        P("shard"),
        P("shard"),
        P("shard"),
        P("shard"),
        P("shard"),
        P("shard"),
        P("shard"),
    )
    return jax.shard_map(local, mesh=mesh, in_specs=in_specs, out_specs=out_specs, check_vma=False)
```

profile of v0, /device:TPU:0, one launch (start us, length us, event | category | flops | bytes accessed | tf_op | source)
XLA Modules:
  0.0 1376.7 jit_solution(11595395446563708483)
XLA Ops:
  18.2 30.6 %all-reduce.18 = (bf16[768]{0:T(1024)(128)(2,1)S(1)}, bf16[768]{0:T(1024)(128)(2,1)S(1)}, bf16[768]{0:T(1024)(128)(2,1)S(1)}, bf16[768]{0:T(1024)(128)(2,1)S(1)}...) all-reduce(bf16[768]{0:T(1024)(128)(2,1)S(1)} %dynamic-update-slice, ...), channel_id=1, replica_groups=mesh['rep'=4,'shard'=8] {'shard'}, use_global_device_ids=true, to_apply=%add | all-reduce | flops 6144 | bytes 24576
  53.9 5.3 all-gather.18.cloned.1.call-done
  70.3 12.7 all-gather
  93.8 35.4 %all-gather.28.cloned.1.call-done = bf16[2048,768]{1,0:T(8,128)(2,1)} async-done(((bf16[512,768]{1,0:T(8,128)(2,1)}), bf16[2048,768]{1,0:T(8,128)(2,1)}) %all-gather.28.cloned.1.call-update) | async-done | bytes 3145744 | tf_op jit(solution)/shard_map/all_gather | solution.py:269
  135.1 40.4 %all-gather.14.cloned.1.call-done = bf16[2048,768]{1,0:T(8,128)(2,1)} async-done(((bf16[512,768]{1,0:T(8,128)(2,1)}), bf16[2048,768]{1,0:T(8,128)(2,1)}) %all-gather.14.cloned.1.call-update) | async-done | bytes 3145744 | tf_op jit(solution)/shard_map/all_gather | solution.py:269
  195.3 25.8 %all-gather.30.cloned.1.call-done = bf16[2048,768]{1,0:T(8,128)(2,1)} async-done(((bf16[512,768]{1,0:T(8,128)(2,1)}), bf16[2048,768]{1,0:T(8,128)(2,1)}) %all-gather.30.cloned.1.call-update) | async-done | bytes 3145744 | tf_op jit(solution)/shard_map/all_gather | solution.py:268
  234.0 33.0 %all-gather.20.cloned.1.call-done = bf16[2048,768]{1,0:T(8,128)(2,1)} async-done(((bf16[512,768]{1,0:T(8,128)(2,1)}), bf16[2048,768]{1,0:T(8,128)(2,1)}) %all-gather.20.cloned.1.call-update) | async-done | bytes 3145744 | tf_op jit(solution)/shard_map/all_gather | solution.py:268
  279.8 7.9 fusion.215
  287.7 6.7 fusion.212
  294.4 7.5 fusion.213
  301.9 6.6 fusion.214
  308.6 17.5 %fusion.5 = f32[12,512]{1,0:T(8,128)S(1)} fusion(f32[12,512]{1,0:T(8,128)S(1)} %maximum_maximum_fusion, f32[12,512,512]{1,2,0:T(8,128)} %get-tuple-element.199, f32[12,512,512]{1,2,0:T(8,128)} %get-tuple-element.201, f32[12,512,512]{1,2,0:T(8,128)} %get-tuple-element.205, f32[12,512,512]{1,2,0:T(8,128)} %get-tuple-element.203), kind=kLoop, calls=%fused_computation.19 | loop fusion | flops 62908416 | bytes 50380800 | tf_op jit(solution)/shard_map/reduce_sum | solution.py:78
  326.2 7.6 fusion.209
  333.8 6.6 fusion.206
  340.4 6.6 fusion.207
  347.1 7.1 fusion.208
  354.2 17.3 %fusion.4 = f32[12,512]{1,0:T(8,128)S(1)} fusion(f32[12,512]{1,0:T(8,128)S(1)} %maximum_maximum_fusion.1, f32[12,512,512]{1,2,0:T(8,128)} %get-tuple-element.187, f32[12,512,512]{1,2,0:T(8,128)} %get-tuple-element.189, f32[12,512,512]{1,2,0:T(8,128)} %get-tuple-element.193, f32[12,512,512]{1,2,0:T(8,128)} %get-tuple-element.191), kind=kLoop, calls=%fused_computation.18 | loop fusion | flops 62908416 | bytes 50380800 | tf_op jit(solution)/shard_map/reduce_sum | solution.py:78
  371.5 39.4 %fusion.6 = (bf16[12,512,2048]{1,2,0:T(8,128)(2,1)}, bf16[12,512,2048]{1,2,0:T(8,128)(2,1)}) fusion(f32[12,512]{1,0:T(8,128)S(1)} %log_add_fusion.1, f32[12,512,512]{1,2,0:T(8,128)} %get-tuple-element.187, f32[12,512,512]{1,2,0:T(8,128)} %get-tuple-element.189, f32[12,512,512]{1,2,0:T(8,128)} %get-tuple-element.193, f32[12,512,512]{1,2,0:T(8,128)} %get-tuple-element.191, ...), kind=kLoop, calls=%fused_computation.20 | loop fusion | flops 100663296 | bytes 100737024 | tf_op jit(solution)/shard_map/convert_element_type | solution.py:116
  431.1 39.2 %fusion.9 = (bf16[12,512,2048]{1,2,0:T(8,128)(2,1)}, bf16[12,512,2048]{1,2,0:T(8,128)(2,1)}) fusion(f32[12,512]{1,0:T(8,128)S(1)} %log_add_fusion, f32[12,512,512]{1,2,0:T(8,128)} %get-tuple-element.199, f32[12,512,512]{1,2,0:T(8,128)} %get-tuple-element.201, f32[12,512,512]{1,2,0:T(8,128)} %get-tuple-element.205, f32[12,512,512]{1,2,0:T(8,128)} %get-tuple-element.203, ...), kind=kLoop, calls=%fused_computation.21 | loop fusion | flops 100663296 | bytes 100737024 | tf_op jit(solution)/shard_map/convert_element_type | solution.py:116
  488.1 8.4 fusion.190
  496.5 7.9 fusion.211
  522.8 18.1 %convert_reduce_fusion.1 = (f32[3072]{0:T(1024)}, bf16[512,3072]{1,0:T(8,128)(2,1)}, f32[3072]{0:T(1024)}, bf16[512,3072]{1,0:T(8,128)(2,1)S(1)}) fusion(f32[512,3072]{1,0:T(8,128)} %fusion.190, f32[3072]{0:T(1024)S(1)} %bitcast.362, f32[512,3072]{1,0:T(8,128)} %fusion.223, f32[512,3072]{1,0:T(8,128)} %copy-done.124, ...), kind=kOutput, calls=%fused_computation.87 | convolution fusion | flops 2488264704 | bytes 30707712 | tf_op jit(solution)/shard_map/dot_general | solution.py:33
  578.9 5.4 fusion.125
  589.1 5.1 fusion.119
  602.2 6.5 fusion.221
  608.7 6.4 fusion.220
  615.1 6.4 fusion.219
  621.4 7.0 fusion.218
  629.2 76.6 %multiply_convert_fusion.1 = bf16[12,512,2048]{1,2,0:T(8,128)(2,1)} fusion(f32[12,512,512]{1,2,0:T(8,128)} %fusion.221, f32[12,512,512]{1,2,0:T(8,128)} %fusion.220, f32[12,512,512]{1,2,0:T(8,128)} %fusion.219, f32[12,512,512]{1,2,0:T(8,128)} %fusion.218, f32[12,512]{1,0:T(8,128)S(1)} %copy-done.86, f32[12,512,512]{1,2,0:T(8,128)} %get-tuple-element.187, ...), kind=kOutput, calls=%fused_computation.10 | output fusion | flops 226500608 | bytes 125853696 | tf_op jit(solution)/shard_map/sub | solution.py:127
  728.0 6.4 fusion.227
  734.3 6.4 fusion.226
  740.7 6.3 fusion.225
  747.1 6.4 fusion.224
  754.2 87.6 %multiply_convert_fusion = bf16[12,512,2048]{1,2,0:T(8,128)(2,1)} fusion(f32[12,512,512]{1,2,0:T(8,128)} %fusion.227, f32[12,512,512]{1,2,0:T(8,128)} %fusion.226, f32[12,512,512]{1,2,0:T(8,128)} %fusion.225, f32[12,512,512]{1,2,0:T(8,128)} %fusion.224, f32[12,512]{1,0:T(8,128)S(1)} %copy-done.84, f32[12,512,512]{1,2,0:T(8,128)} %get-tuple-element.199, ...), kind=kOutput, calls=%fused_computation.6 | output fusion | flops 226500608 | bytes 125853696 | tf_op jit(solution)/shard_map/sub | solution.py:127
  868.5 4.9 fusion.78
  921.2 13.1 reduce-scatter.21.cloned.1.call-done
  942.1 6.0 fusion.192
  948.2 10.2 convolution_add_fusion
  959.8 5.0 fusion.188
  964.9 5.9 convolution_add_fusion.1
  983.1 27.4 %reduce-scatter.31.cloned.1.call-done = f32[96,768]{1,0:T(8,128)} async-done(((f32[768,768]{1,0:T(8,128)}), f32[96,768]{1,0:T(8,128)}) %reduce-scatter.31.cloned.1.call-update) | async-done | bytes 294928
  1012.4 35.7 %reduce-scatter.35.cloned.1.call-done = f32[96,768]{1,0:T(8,128)} async-done(((f32[768,768]{1,0:T(8,128)}), f32[96,768]{1,0:T(8,128)}) %reduce-scatter.35.cloned.1.call-update) | async-done | bytes 294928
  1049.9 35.8 %reduce-scatter.33.cloned.1.call-done = f32[96,768]{1,0:T(8,128)} async-done(((f32[768,768]{1,0:T(8,128)}), f32[96,768]{1,0:T(8,128)}) %reduce-scatter.33.cloned.1.call-update) | async-done | bytes 294928
  1087.5 99.2 %reduce-scatter.29.cloned.1.call-done = f32[384,768]{1,0:T(8,128)} async-done(((f32[3072,768]{1,0:T(8,128)}), f32[384,768]{1,0:T(8,128)}) %reduce-scatter.29.cloned.1.call-update) | async-done | bytes 1179664 | tf_op jit(solution)/shard_map/reduce_scatter | solution.py:380
  1188.9 97.9 %reduce-scatter.27.cloned.1.call-done = f32[96,3072]{1,0:T(8,128)} async-done(((f32[768,3072]{1,0:T(8,128)}), f32[96,3072]{1,0:T(8,128)}) %reduce-scatter.27.cloned.1.call-update) | async-done | bytes 1179664 | tf_op jit(solution)/shard_map/reduce_scatter | solution.py:380
  1289.2 26.4 %all-reduce.17 = (bf16[768]{0:T(1024)(128)(2,1)S(1)}, bf16[768]{0:T(1024)(128)(2,1)S(1)}, bf16[768]{0:T(1024)(128)(2,1)S(1)}, bf16[3072]{0:T(1024)(128)(2,1)S(1)...) all-reduce(f32[768]{0:T(1024)S(1)} %add.445, ...), channel_id=12, replica_groups=mesh['rep'=4,'shard'=8] {'shard'}, use_global_device_ids=true, to_apply=%region_46.47.clone | all-reduce | flops 9216 | bytes 55296
  1316.3 10.0 all-reduce.19
  1340.1 18.0 %all-reduce.23.cloned.1.call-done = (bf16[96,768]{0,1:T(8,128)(2,1)}, bf16[96,768]{0,1:T(8,128)(2,1)}, bf16[96,768]{0,1:T(8,128)(2,1)}, bf16[96,768]{1,0:T(8,128...) async-done(((bf16[96,768]{0,1:T(8,128)(2,1)}, bf16[96,768]{0,1:T(8,128)(2,1)}, bf16[96,768]{0,1:T(8,128)(2,1)}, bf16[96,768]{1,0:T(8,128)(2,1)}, ...) | async-done | bytes 1769488 | tf_op jit(solution)/shard_map/psum | solution.py:381
  (518 shorter events, 347.9 us)
Async XLA Ops:
  7.2 44.9 %copy-start.9 = (bf16[2,512,768]{2,1,0:T(8,128)(2,1)S(1)}, bf16[2,512,768]{2,1,0:T(8,128)(2,1)}, u32[]{:S(2)}) copy-start(bf16[2,512,768]{2,1,0:T(8,128)(2,1)} %param.18) | copy-start | bytes 4718596
  7.2 41.5 %all-gather.12.cloned.1.call-start = ((), (), s32[]{:S(2)}) async-start(), calls=%async_computation.10 | async-start | bytes 1327104 | tf_op jit(solution)/shard_map/all_gather | solution.py:232
  7.9 51.3 %all-gather.18.cloned.1.call-start = ((), (), s32[]{:S(2)}) async-start(), calls=%async_computation.13 | async-start | bytes 1327104 | tf_op jit(solution)/shard_map/all_gather | solution.py:231
  8.7 78.0 %all-gather.16.cloned.1.call-start = ((), (), s32[]{:S(2)}) async-start(), calls=%async_computation.12 | async-start | bytes 1327104 | tf_op jit(solution)/shard_map/all_gather | solution.py:230
  9.4 119.8 %all-gather.28.cloned.1.call-start = ((), (), s32[]{:S(2)}) async-start(), calls=%async_computation.18 | async-start | bytes 3932160 | tf_op jit(solution)/shard_map/all_gather | solution.py:269
  52.1 123.4 %all-gather.14.cloned.1.call-start = ((), (), s32[]{:S(2)}) async-start(), calls=%async_computation.11 | async-start | bytes 3932160 | tf_op jit(solution)/shard_map/all_gather | solution.py:269
  53.8 13.5 copy-start.89
  53.8 13.5 copy-start.119
  53.8 167.3 %all-gather.30.cloned.1.call-start = ((), (), s32[]{:S(2)}) async-start(), calls=%async_computation.19 | async-start | bytes 3932160 | tf_op jit(solution)/shard_map/all_gather | solution.py:268
  62.2 204.8 %all-gather.20.cloned.1.call-start = ((), (), s32[]{:S(2)}) async-start(), calls=%async_computation.14 | async-start | bytes 3932160 | tf_op jit(solution)/shard_map/all_gather | solution.py:268
  65.2 362.0 %all-gather.22.cloned.1.call-start = ((), (), s32[]{:S(2)}) async-start(), calls=%async_computation.15 | async-start | bytes 1327104 | tf_op jit(solution)/shard_map/all_gather | solution.py:233
  65.9 422.2 %all-gather.24.cloned.1.call-start = ((), (), s32[]{:S(2)}) async-start(), calls=%async_computation.16 | async-start | bytes 5308416 | tf_op jit(solution)/shard_map/all_gather | solution.py:234
  66.7 429.8 %all-gather.26.cloned.1.call-start = ((), (), s32[]{:S(2)}) async-start(), calls=%async_computation.17 | async-start | bytes 5308416 | tf_op jit(solution)/shard_map/all_gather | solution.py:235
  67.3 838.9 %reduce-scatter.19.cloned.1.call-start = ((), (), s32[]{:S(2)}) async-start(), calls=%async_computation.21 | async-start | bytes 7864320 | tf_op jit(solution)/shard_map/reduce_scatter | solution.py:345
  89.1 212.9 %copy-start = (bf16[512,768]{0,1:T(8,128)(2,1)}, bf16[512,768]{0,1:T(8,128)(2,1)S(1)}, u32[]{:S(2)}) copy-start(bf16[512,768]{0,1:T(8,128)(2,1)S(1)} %copy.203) | copy-start | bytes 2359300
  93.8 253.3 %copy-start.2 = (bf16[512,768]{0,1:T(8,128)(2,1)}, bf16[512,768]{0,1:T(8,128)(2,1)S(1)}, u32[]{:S(2)}) copy-start(bf16[512,768]{0,1:T(8,128)(2,1)S(1)} %copy.190) | copy-start | bytes 2359300
  308.6 17.6 %copy-start.23 = (bf16[512,768]{0,1:T(8,128)(2,1)S(1)}, bf16[512,768]{0,1:T(8,128)(2,1)}, u32[]{:S(2)}) copy-start(bf16[512,768]{0,1:T(8,128)(2,1)} %copy.192) | copy-start | bytes 2359300
  326.1 105.0 %copy-start.83 = (f32[12,512]{1,0:T(8,128)}, f32[12,512]{1,0:T(8,128)S(1)}, u32[]{:S(2)}) copy-start(f32[12,512]{1,0:T(8,128)S(1)} %log_add_fusion) | copy-start | bytes 73732
  371.5 39.4 %copy-start.85 = (f32[12,512]{1,0:T(8,128)}, f32[12,512]{1,0:T(8,128)S(1)}, u32[]{:S(2)}) copy-start(f32[12,512]{1,0:T(8,128)S(1)} %log_add_fusion.1) | copy-start | bytes 73732
  371.5 39.4 %copy-start.43 = (bf16[512,768]{0,1:T(8,128)(2,1)S(1)}, bf16[512,768]{0,1:T(8,128)(2,1)}, u32[]{:S(2)}) copy-start(bf16[512,768]{0,1:T(8,128)(2,1)} %copy.200) | copy-start | bytes 2359300
  427.2 43.1 %copy-start.62 = (bf16[12,64,512]{2,1,0:T(8,128)(2,1)}, bf16[12,64,512]{2,1,0:T(8,128)(2,1)S(1)}, u32[]{:S(2)}) copy-start(bf16[12,64,512]{2,1,0:T(8,128)(2,1)S(1)} %add_convert_fusion.7) | copy-start | bytes 2359300
  429.7 118.3 %copy-start.95 = (f32[512]{0:T(512)}, f32[512]{0:T(512)S(1)}, u32[]{:S(2)}) copy-start(f32[512]{0:T(512)S(1)} %broadcast_multiply_fusion.3) | copy-start | bytes 6148
  431.1 39.2 %copy-start.35 = (bf16[512,768]{0,1:T(8,128)(2,1)S(1)}, bf16[512,768]{0,1:T(8,128)(2,1)}, u32[]{:S(2)}) copy-start(bf16[512,768]{0,1:T(8,128)(2,1)} %copy.213) | copy-start | bytes 2359300
  487.7 60.4 %copy-start.6 = (f32[512,768]{1,0:T(8,128)}, f32[512,768]{1,0:T(8,128)S(1)}, u32[]{:S(2)}) copy-start(f32[512,768]{1,0:T(8,128)S(1)} %get-tuple-element.207) | copy-start | bytes 4718596
  487.7 60.4 %copy-start.90 = (f32[512]{0:T(512)}, f32[512]{0:T(512)S(1)}, u32[]{:S(2)}) copy-start(f32[512]{0:T(512)S(1)} %broadcast_multiply_fusion.1) | copy-start | bytes 6148
  488.0 60.0 %copy-start.112 = (f32[512]{0:T(512)}, f32[512]{0:T(512)S(1)}, u32[]{:S(2)}) copy-start(f32[512]{0:T(512)S(1)} %fusion.175) | copy-start | bytes 6148
  488.0 60.0 %copy-start.93 = (f32[512]{0:T(512)}, f32[512]{0:T(512)S(1)}, u32[]{:S(2)}) copy-start(f32[512]{0:T(512)S(1)} %fusion.177) | copy-start | bytes 6148
  549.6 25.2 %copy-start.12 = (f32[512,768]{1,0:T(8,128)}, f32[512,768]{1,0:T(8,128)S(1)}, u32[]{:S(2)}) copy-start(f32[512,768]{1,0:T(8,128)S(1)} %get-tuple-element.172) | copy-start | bytes 4718596
  574.7 335.0 %reduce-scatter.23.cloned.1.call-start = ((), (), s32[]{:S(2)}) async-start(), calls=%async_computation.23 | async-start | bytes 7864320 | tf_op jit(solution)/shard_map/reduce_scatter | solution.py:345
  578.8 15.3 %copy-start.4 = (bf16[512,768]{0,1:T(8,128)(2,1)}, bf16[512,768]{0,1:T(8,128)(2,1)S(1)}, u32[]{:S(2)}) copy-start(bf16[512,768]{0,1:T(8,128)(2,1)S(1)} %copy.228) | copy-start | bytes 2359300
  628.5 77.3 %copy-start.3 = (bf16[512,768]{0,1:T(8,128)(2,1)S(1)}, bf16[512,768]{0,1:T(8,128)(2,1)}, u32[]{:S(2)}) copy-start(bf16[512,768]{0,1:T(8,128)(2,1)} %copy-done.2) | copy-start | bytes 2359300
  628.5 289.1 %reduce-scatter.17.cloned.1.call-start = ((), (), s32[]{:S(2)}) async-start(), calls=%async_computation.20 | async-start | bytes 7864320 | tf_op jit(solution)/shard_map/reduce_scatter | solution.py:339
  753.5 88.3 %copy-start.1 = (bf16[512,768]{0,1:T(8,128)(2,1)S(1)}, bf16[512,768]{0,1:T(8,128)(2,1)}, u32[]{:S(2)}) copy-start(bf16[512,768]{0,1:T(8,128)(2,1)} %copy-done) | copy-start | bytes 2359300
  753.5 180.9 %reduce-scatter.21.cloned.1.call-start = ((), (), s32[]{:S(2)}) async-start(), calls=%async_computation.22 | async-start | bytes 7864320 | tf_op jit(solution)/shard_map/reduce_scatter | solution.py:339
  864.0 117.3 %reduce-scatter.25.cloned.1.call-start = ((), (), s32[]{:S(2)}) async-start(), calls=%async_computation.24 | async-start | bytes 2654208 | tf_op jit(solution)/shard_map/reduce_scatter | solution.py:380
  868.4 142.1 %reduce-scatter.31.cloned.1.call-start = ((), (), s32[]{:S(2)}) async-start(), calls=%async_computation.27 | async-start | bytes 2654208
  868.4 24.8 %slice-start = ((s8[25165824]{0:T(1024)(128)(4,1)}), s8[4194304]{0:T(1024)(128)(4,1)S(1)}, s32[]{:S(2)}) async-start(s8[25165824]{0:T(1024)(128)(4,1)} %bitcast.276), calls=%async_computation.31 | async-start | bytes 8388608
  868.5 24.8 %slice-start.1 = ((s8[25165824]{0:T(1024)(128)(4,1)}), s8[4194304]{0:T(1024)(128)(4,1)S(1)}, s32[]{:S(2)}) async-start(s8[25165824]{0:T(1024)(128)(4,1)} %bitcast.276), calls=%async_computation.32 | async-start | bytes 8388608
  873.4 19.9 %slice-start.2 = ((s8[25165824]{0:T(1024)(128)(4,1)}), s8[4194304]{0:T(1024)(128)(4,1)S(1)}, s32[]{:S(2)}) async-start(s8[25165824]{0:T(1024)(128)(4,1)} %bitcast.276), calls=%async_computation.33 | async-start | bytes 8388608
  878.1 15.1 %slice-start.3 = ((s8[25165824]{0:T(1024)(128)(4,1)}), s8[4194304]{0:T(1024)(128)(4,1)S(1)}, s32[]{:S(2)}) async-start(s8[25165824]{0:T(1024)(128)(4,1)} %bitcast.276), calls=%async_computation.34 | async-start | bytes 8388608
  906.1 142.1 %reduce-scatter.35.cloned.1.call-start = ((), (), s32[]{:S(2)}) async-start(), calls=%async_computation.29 | async-start | bytes 2654208
  917.5 168.2 %reduce-scatter.33.cloned.1.call-start = ((), (), s32[]{:S(2)}) async-start(), calls=%async_computation.28 | async-start | bytes 2654208
  941.9 244.9 %reduce-scatter.29.cloned.1.call-start = ((), (), s32[]{:S(2)}) async-start(), calls=%async_computation.26 | async-start | bytes 10616832 | tf_op jit(solution)/shard_map/reduce_scatter | solution.py:380
  958.4 328.4 %reduce-scatter.27.cloned.1.call-start = ((), (), s32[]{:S(2)}) async-start(), calls=%async_computation.25 | async-start | bytes 10616832 | tf_op jit(solution)/shard_map/reduce_scatter | solution.py:380
  970.9 387.3 %all-reduce.23.cloned.1.call-start = ((), (), s32[]{:S(2)}) async-start(), calls=%async_computation.30 | async-start | bytes 3833856 | tf_op jit(solution)/shard_map/psum | solution.py:381
  974.6 37.7 %copy-start.11 = (f32[512,768]{0,1:T(8,128)S(1)}, f32[512,768]{0,1:T(8,128)}, u32[]{:S(2)}) copy-start(f32[512,768]{0,1:T(8,128)} %reduce-scatter.19.cloned.1.call-done) | copy-start | bytes 4718596
  981.3 307.7 %copy-start.8 = (f32[512,768]{0,1:T(8,128)S(1)}, f32[512,768]{0,1:T(8,128)}, u32[]{:S(2)}) copy-start(f32[512,768]{0,1:T(8,128)} %reduce-scatter.23.cloned.1.call-done) | copy-start | bytes 4718596
  1289.2 46.6 %copy-start.98 = (f32[512]{0:T(512)S(1)}, f32[512]{0:T(512)}, u32[]{:S(2)}) copy-start(f32[512]{0:T(512)} %copy-done.97) | copy-start | bytes 6148
  (107 other events, 435.7 us)
Sparse Core Ops, SparseCore 0:
  9.7 25.5 all-gather.11
  36.9 22.3 all-gather.17
  60.9 22.3 all-gather.15
  85.5 43.6 all-gather.27
  131.4 43.9 all-gather.13
  177.2 43.9 all-gather.29
  223.0 43.9 all-gather.19
  268.7 22.6 all-gather.21
  293.0 51.4 all-gather.23
  346.0 50.5 all-gather.25
  574.8 70.3 reduce-scatter.18
  648.1 70.1 reduce-scatter.22
  753.6 70.1 reduce-scatter.16
  864.1 70.2 reduce-scatter.20
  936.5 36.3 reduce-scatter.24
  975.1 35.3 reduce-scatter.30
  1012.6 35.4 reduce-scatter.34
  1050.3 35.3 reduce-scatter.32
  1088.1 98.6 reduce-scatter.28
  1188.9 97.8 reduce-scatter.26
  1291.3 66.8 all-reduce.22
where the time goes:
time: 1380 us
  waiting for transfers between devices  472 us (34%)
  matrix products  385 us (28%)
  other arithmetic  327 us (24%)
  local copies, waits for them, and re-layouts  93.1 us (7%)
  blocking collectives  79.7 us (6%)
  between operations  19 us (1%)
    reduce_scatter x3, waiting for transfers between devices, local(): summed = lax.psum_scatter(totals, 'shard', scatter_dimension=0, tiled=True)  197 us
    sub x2, other arithmetic, attend_backward(): grad_scores = (chances * (grad_chances - centre)).astype(jnp.bfloat16)  164 us
    unnamed x24, waiting for transfers between devices  103 us
    convert_element_type x2, other arithmetic, attend_backward(): chance_low = chances.astype(jnp.bfloat16)  78.5 us
    all_gather x2, waiting for transfers between devices, local(): lax.all_gather(values_local, 'rep', axis=0, tiled=True)  75.8 us
    all_gather x2, waiting for transfers between devices, local(): lax.all_gather(keys_local, 'rep', axis=0, tiled=True)  58.8 us
    unnamed x2, blocking collectives  57 us
    dot_general x8, matrix products, block_scores(): unmasked = product()  56.7 us
  transfers between devices with their start and end apart: 21, of which 12 were waited for; matrix products, arithmetic and copies ran while one was open for 51% of the time, Pallas kernels for 0%

commit v1 on v0

--- a/solution.py
+++ b/solution.py
@@ -7,6 +7,19 @@
 HEAD_DIM = 64
 masked_value = -1e30
 norm_eps = 1e-05
+
+
+def gather_around(x, axis, dim):
+    count, position, extent = (lax.axis_size(axis), lax.axis_index(axis), x.shape[dim])
+    forward = [(i, (i + 1) % count) for i in range(count)]
+    out = jnp.zeros((*x.shape[:dim], count * extent, *x.shape[dim + 1 :]), x.dtype)
+    held = x
+    for step in range(count):
+        owner = (position - step) % count
+        out = lax.dynamic_update_slice_in_dim(out, held, owner * extent, axis=dim)
+        if step < count - 1:
+            held = lax.ppermute(held, axis, forward)
+    return out
 
 
 def as_sent(array):
@@ -266,7 +279,7 @@
         values_local = (dense(inputs_now, value_matrix) + value_vector).astype(jnp.bfloat16)
         keys_whole, values_whole = (
             lax.all_gather(keys_local, "rep", axis=0, tiled=True),
-            lax.all_gather(values_local, "rep", axis=0, tiled=True),
+            gather_around(values_local, "rep", 0),
         )
         mixture, logsums = attend_forward(
             heads_of(queries),

time: 1380 us -> 1370 us (level)
  waiting for transfers between devices: 472 us -> 441 us
    ppermute x0 -> x6, waiting for transfers between devices: none -> 84.6 us  [gather_around(): held = lax.ppermute(held, axis, forward)]
    all_gather x2 -> x0, waiting for transfers between devices: 75.8 us -> none  [local(): lax.all_gather(values_local, 'rep', axis=0, tiled=True)]
    all_gather x2, waiting for transfers between devices: 58.8 us -> 0.01 us  [local(): lax.all_gather(keys_local, 'rep', axis=0, tiled=True)]
    all_gather x1, waiting for transfers between devices: 5.35 us -> 25.5 us  [local(): lax.all_gather(shards[1], 'shard', axis=0, tiled=True)]
    slice x10 -> x2, local copies, waits for them, and re-layouts: 25.7 us -> 7.32 us  [attend_forward(): value_block = value_heads[number * block_rows:(number + 1) * block_rows]]
    dynamic_update_slice x0 -> x7, local copies, waits for them, and re-layouts: none -> 14.3 us  [gather_around(): out = lax.dynamic_update_slice_in_dim(out, held, owner * extent, axis=dim)]
    unnamed x304 -> x322, local copies, waits for them, and re-layouts: 39.3 us -> 33.3 us
    unnamed x24 -> x22, waiting for transfers between devices: 103 us -> 103 us
  transfers between devices with their start and end apart: 21 -> 25, of which waited for: 12 -> 13; matrix products, arithmetic and copies ran while one was open for 51% -> 52% of each run, Pallas kernels for 0% -> 0%
where the time goes in v1:
time: 1370 us; the launch traced here: 1360 us
  waiting for transfers between devices  441 us (32%)
  matrix products  384 us (28%)
  other arithmetic  326 us (24%)
  local copies, waits for them, and re-layouts  103 us (8%)
  blocking collectives  77 us (6%)
  between operations  18.9 us (1%)
    reduce_scatter x3, waiting for transfers between devices, local(): summed = lax.psum_scatter(totals, 'shard', scatter_dimension=0, tiled=True)  197 us
    sub x2, other arithmetic, attend_backward(): grad_scores = (chances * (grad_chances - centre)).astype(jnp.bfloat16)  164 us
    unnamed x22, waiting for transfers between devices  103 us
    ppermute x6, waiting for transfers between devices, gather_around(): held = lax.ppermute(held, axis, forward)  84.6 us
    convert_element_type x2, other arithmetic, attend_backward(): chance_low = chances.astype(jnp.bfloat16)  78.4 us
    dot_general x8, matrix products, block_scores(): unmasked = product()  55.9 us
    unnamed x2, blocking collectives  54.3 us
    dot_general x8, matrix products, attend_backward(): pieces.append(product())  51.3 us
  transfers between devices with their start and end apart: 25, of which 13 were waited for; matrix products, arithmetic and copies ran while one was open for 52% of the time, Pallas kernels for 0%

profile of v1, /device:TPU:0, one launch (start us, length us, event | category | flops | bytes accessed | tf_op | source)
XLA Modules:
  0.0 1360.1 jit_solution(6395063207070383596)
XLA Ops:
  9.6 25.5 %all-gather.14.cloned.1.call-done = bf16[768,768]{1,0:T(8,128)(2,1)} async-done(((bf16[96,768]{1,0:T(8,128)(2,1)}), bf16[768,768]{1,0:T(8,128)(2,1)}) %all-gather.14.cloned.1.call-update) | async-done | bytes 1179664 | tf_op jit(solution)/shard_map/all_gather | solution.py:244
  46.6 27.9 %all-reduce.18 = (bf16[768]{0:T(1024)(128)(2,1)S(1)}, bf16[768]{0:T(1024)(128)(2,1)S(1)}, bf16[768]{0:T(1024)(128)(2,1)S(1)}, bf16[768]{0:T(1024)(128)(2,1)S(1)}...) all-reduce(bf16[768]{0:T(1024)(128)(2,1)S(1)} %dynamic-update-slice, ...), channel_id=1, replica_groups=mesh['rep'=4,'shard'=8] {'shard'}, use_global_device_ids=true, to_apply=%add | all-reduce | flops 6144 | bytes 24576
  84.8 12.7 all-gather
  101.8 24.1 %collective-permute-done.3 = bf16[512,768]{1,0:T(8,128)(2,1)} collective-permute-done((bf16[512,768]{1,0:T(8,128)(2,1)S(1)}, bf16[512,768]{1,0:T(8,128)(2,1)}, u32[]{:S(2)}, u32[]{:S(2)}) %collective-permute-start.3) | collective-permute-done | bytes 786464 | tf_op jit(solution)/shard_map/ppermute | solution.py:21
  138.4 18.7 %collective-permute-done.1 = bf16[512,768]{1,0:T(8,128)(2,1)} collective-permute-done((bf16[512,768]{1,0:T(8,128)(2,1)}, bf16[512,768]{1,0:T(8,128)(2,1)}, u32[]{:S(2)}, u32[]{:S(2)}) %collective-permute-start.1) | collective-permute-done | bytes 786464 | tf_op jit(solution)/shard_map/ppermute | solution.py:21
  157.7 23.1 %collective-permute-done.4 = bf16[512,768]{1,0:T(8,128)(2,1)} collective-permute-done((bf16[512,768]{1,0:T(8,128)(2,1)}, bf16[512,768]{1,0:T(8,128)(2,1)}, u32[]{:S(2)}, u32[]{:S(2)}) %collective-permute-start.4) | collective-permute-done | bytes 786464 | tf_op jit(solution)/shard_map/ppermute | solution.py:21
  210.2 18.2 %collective-permute-done.5 = bf16[512,768]{1,0:T(8,128)(2,1)} collective-permute-done((bf16[512,768]{1,0:T(8,128)(2,1)}, bf16[512,768]{1,0:T(8,128)(2,1)}, u32[]{:S(2)}, u32[]{:S(2)}) %collective-permute-start.5) | collective-permute-done | bytes 786464 | tf_op jit(solution)/shard_map/ppermute | solution.py:21
  266.4 7.9 fusion.215
  274.3 6.7 fusion.212
  281.0 6.6 fusion.213
  287.6 7.1 fusion.214
  294.8 17.6 %fusion.5 = f32[12,512]{1,0:T(8,128)S(1)} fusion(f32[12,512]{1,0:T(8,128)S(1)} %maximum_maximum_fusion, f32[12,512,512]{1,2,0:T(8,128)} %get-tuple-element.199, f32[12,512,512]{1,2,0:T(8,128)} %get-tuple-element.201, f32[12,512,512]{1,2,0:T(8,128)} %get-tuple-element.205, f32[12,512,512]{1,2,0:T(8,128)} %get-tuple-element.203), kind=kLoop, calls=%fused_computation.19 | loop fusion | flops 62908416 | bytes 50380800 | tf_op jit(solution)/shard_map/reduce_sum | solution.py:91
  312.5 7.7 fusion.209
  320.1 6.6 fusion.206
  326.7 6.7 fusion.207
  333.4 6.7 fusion.208
  340.1 17.2 %fusion.4 = f32[12,512]{1,0:T(8,128)S(1)} fusion(f32[12,512]{1,0:T(8,128)S(1)} %maximum_maximum_fusion.1, f32[12,512,512]{1,2,0:T(8,128)} %get-tuple-element.187, f32[12,512,512]{1,2,0:T(8,128)} %get-tuple-element.189, f32[12,512,512]{1,2,0:T(8,128)} %get-tuple-element.193, f32[12,512,512]{1,2,0:T(8,128)} %get-tuple-element.191), kind=kLoop, calls=%fused_computation.18 | loop fusion | flops 62908416 | bytes 50380800 | tf_op jit(solution)/shard_map/reduce_sum | solution.py:91
  357.4 39.3 %fusion.6 = (bf16[12,512,2048]{1,2,0:T(8,128)(2,1)}, bf16[12,512,2048]{1,2,0:T(8,128)(2,1)}) fusion(f32[12,512]{1,0:T(8,128)S(1)} %log_add_fusion.1, f32[12,512,512]{1,2,0:T(8,128)} %get-tuple-element.187, f32[12,512,512]{1,2,0:T(8,128)} %get-tuple-element.189, f32[12,512,512]{1,2,0:T(8,128)} %get-tuple-element.193, f32[12,512,512]{1,2,0:T(8,128)} %get-tuple-element.191, ...), kind=kLoop, calls=%fused_computation.20 | loop fusion | flops 100663296 | bytes 100737024 | tf_op jit(solution)/shard_map/convert_element_type | solution.py:129
  416.9 39.2 %fusion.9 = (bf16[12,512,2048]{1,2,0:T(8,128)(2,1)}, bf16[12,512,2048]{1,2,0:T(8,128)(2,1)}) fusion(f32[12,512]{1,0:T(8,128)S(1)} %log_add_fusion, f32[12,512,512]{1,2,0:T(8,128)} %get-tuple-element.199, f32[12,512,512]{1,2,0:T(8,128)} %get-tuple-element.201, f32[12,512,512]{1,2,0:T(8,128)} %get-tuple-element.205, f32[12,512,512]{1,2,0:T(8,128)} %get-tuple-element.203, ...), kind=kLoop, calls=%fused_computation.21 | loop fusion | flops 100663296 | bytes 100737024 | tf_op jit(solution)/shard_map/convert_element_type | solution.py:129
  473.8 8.4 fusion.190
  482.2 7.9 fusion.211
  508.5 18.1 %convert_reduce_fusion.1 = (f32[3072]{0:T(1024)}, bf16[512,3072]{1,0:T(8,128)(2,1)}, f32[3072]{0:T(1024)}, bf16[512,3072]{1,0:T(8,128)(2,1)S(1)}) fusion(f32[512,3072]{1,0:T(8,128)} %fusion.190, f32[3072]{0:T(1024)S(1)} %bitcast.362, f32[512,3072]{1,0:T(8,128)} %fusion.223, f32[512,3072]{1,0:T(8,128)} %copy-done.133, ...), kind=kOutput, calls=%fused_computation.87 | convolution fusion | flops 2488264704 | bytes 30707712 | tf_op jit(solution)/shard_map/dot_general | solution.py:46
  564.5 5.8 fusion.125
  580.0 5.2 fusion.116
  588.4 6.5 fusion.221
  594.8 6.4 fusion.220
  601.2 6.4 fusion.219
  607.6 6.4 fusion.218
  614.8 76.6 %multiply_convert_fusion.1 = bf16[12,512,2048]{1,2,0:T(8,128)(2,1)} fusion(f32[12,512,512]{1,2,0:T(8,128)} %fusion.221, f32[12,512,512]{1,2,0:T(8,128)} %fusion.220, f32[12,512,512]{1,2,0:T(8,128)} %fusion.219, f32[12,512,512]{1,2,0:T(8,128)} %fusion.218, f32[12,512]{1,0:T(8,128)S(1)} %copy-done.86, f32[12,512,512]{1,2,0:T(8,128)} %get-tuple-element.187, ...), kind=kOutput, calls=%fused_computation.10 | output fusion | flops 226500608 | bytes 125853696 | tf_op jit(solution)/shard_map/sub | solution.py:140
  696.4 4.9 fusion.84
  713.9 6.4 fusion.227
  720.3 6.4 fusion.226
  726.8 6.3 fusion.225
  733.1 6.4 fusion.224
  740.3 87.0 %multiply_convert_fusion = bf16[12,512,2048]{1,2,0:T(8,128)(2,1)} fusion(f32[12,512,512]{1,2,0:T(8,128)} %fusion.227, f32[12,512,512]{1,2,0:T(8,128)} %fusion.226, f32[12,512,512]{1,2,0:T(8,128)} %fusion.225, f32[12,512,512]{1,2,0:T(8,128)} %fusion.224, f32[12,512]{1,0:T(8,128)S(1)} %copy-done.84, f32[12,512,512]{1,2,0:T(8,128)} %get-tuple-element.199, ...), kind=kOutput, calls=%fused_computation.6 | output fusion | flops 226500608 | bytes 125853696 | tf_op jit(solution)/shard_map/sub | solution.py:140
  905.6 12.4 reduce-scatter.21.cloned.1.call-done
  925.8 6.0 fusion.192
  931.8 10.2 convolution_add_fusion
  943.5 5.0 fusion.188
  948.5 5.7 convolution_add_fusion.1
  966.6 27.6 %reduce-scatter.31.cloned.1.call-done = f32[96,768]{1,0:T(8,128)} async-done(((f32[768,768]{1,0:T(8,128)}), f32[96,768]{1,0:T(8,128)}) %reduce-scatter.31.cloned.1.call-update) | async-done | bytes 294928
  996.2 35.7 %reduce-scatter.35.cloned.1.call-done = f32[96,768]{1,0:T(8,128)} async-done(((f32[768,768]{1,0:T(8,128)}), f32[96,768]{1,0:T(8,128)}) %reduce-scatter.35.cloned.1.call-update) | async-done | bytes 294928
  1033.7 35.9 %reduce-scatter.33.cloned.1.call-done = f32[96,768]{1,0:T(8,128)} async-done(((f32[768,768]{1,0:T(8,128)}), f32[96,768]{1,0:T(8,128)}) %reduce-scatter.33.cloned.1.call-update) | async-done | bytes 294928
  1071.4 99.1 %reduce-scatter.29.cloned.1.call-done = f32[384,768]{1,0:T(8,128)} async-done(((f32[3072,768]{1,0:T(8,128)}), f32[384,768]{1,0:T(8,128)}) %reduce-scatter.29.cloned.1.call-update) | async-done | bytes 1179664 | tf_op jit(solution)/shard_map/reduce_scatter | solution.py:393
  1172.6 97.9 %reduce-scatter.27.cloned.1.call-done = f32[96,3072]{1,0:T(8,128)} async-done(((f32[768,3072]{1,0:T(8,128)}), f32[96,3072]{1,0:T(8,128)}) %reduce-scatter.27.cloned.1.call-update) | async-done | bytes 1179664 | tf_op jit(solution)/shard_map/reduce_scatter | solution.py:393
  1272.9 26.4 %all-reduce.17 = (bf16[768]{0:T(1024)(128)(2,1)S(1)}, bf16[768]{0:T(1024)(128)(2,1)S(1)}, bf16[768]{0:T(1024)(128)(2,1)S(1)}, bf16[3072]{0:T(1024)(128)(2,1)S(1)...) all-reduce(f32[768]{0:T(1024)S(1)} %add.489, ...), channel_id=12, replica_groups=mesh['rep'=4,'shard'=8] {'shard'}, use_global_device_ids=true, to_apply=%region_46.47.clone | all-reduce | flops 9216 | bytes 55296
  1300.1 10.0 all-reduce.19
  1323.8 18.0 %all-reduce.23.cloned.1.call-done = (bf16[96,768]{0,1:T(8,128)(2,1)}, bf16[96,768]{0,1:T(8,128)(2,1)}, bf16[96,768]{0,1:T(8,128)(2,1)}, bf16[96,768]{1,0:T(8,128...) async-done(((bf16[96,768]{0,1:T(8,128)(2,1)}, bf16[96,768]{0,1:T(8,128)(2,1)}, bf16[96,768]{0,1:T(8,128)(2,1)}, bf16[96,768]{1,0:T(8,128)(2,1)}, ...) | async-done | bytes 1769488 | tf_op jit(solution)/shard_map/psum | solution.py:394
  (551 shorter events, 366.6 us)
Async XLA Ops:
  7.2 27.9 %all-gather.14.cloned.1.call-start = ((), (), s32[]{:S(2)}) async-start(), calls=%async_computation.12 | async-start | bytes 1327104 | tf_op jit(solution)/shard_map/all_gather | solution.py:244
  7.9 66.6 %all-gather.10.cloned.1.call-start = ((), (), s32[]{:S(2)}) async-start(), calls=%async_computation.10 | async-start | bytes 1327104 | tf_op jit(solution)/shard_map/all_gather | solution.py:245
  8.7 122.8 %all-gather.12.cloned.1.call-start = ((), (), s32[]{:S(2)}) async-start(), calls=%async_computation.11 | async-start | bytes 1327104 | tf_op jit(solution)/shard_map/all_gather | solution.py:243
  9.5 36.5 %copy-start.130 = (bf16[96]{0:T(256)(128)(2,1)S(1)}, bf16[96]{0:T(256)(128)(2,1)}, u32[]{:S(2)}) copy-start(bf16[96]{0:T(256)(128)(2,1)} %param.27) | copy-start | bytes 580
  9.5 36.7 %copy-start.131 = (bf16[96]{0:T(256)(128)(2,1)S(1)}, bf16[96]{0:T(256)(128)(2,1)}, u32[]{:S(2)}) copy-start(bf16[96]{0:T(256)(128)(2,1)} %param.28) | copy-start | bytes 580
  9.5 36.9 %copy-start.132 = (bf16[96]{0:T(256)(128)(2,1)S(1)}, bf16[96]{0:T(256)(128)(2,1)}, u32[]{:S(2)}) copy-start(bf16[96]{0:T(256)(128)(2,1)} %param.35) | copy-start | bytes 580
  9.5 231.1 %all-gather.24.cloned.1.call-start = ((), (), s32[]{:S(2)}) async-start(), calls=%async_computation.17 | async-start | bytes 3932160 | tf_op jit(solution)/shard_map/all_gather | solution.py:281
  38.3 215.2 %all-gather.16.cloned.1.call-start = ((), (), s32[]{:S(2)}) async-start(), calls=%async_computation.13 | async-start | bytes 3932160 | tf_op jit(solution)/shard_map/all_gather | solution.py:281
  41.3 371.6 %all-gather.18.cloned.1.call-start = ((), (), s32[]{:S(2)}) async-start(), calls=%async_computation.14 | async-start | bytes 1327104 | tf_op jit(solution)/shard_map/all_gather | solution.py:246
  41.9 431.9 %all-gather.20.cloned.1.call-start = ((), (), s32[]{:S(2)}) async-start(), calls=%async_computation.15 | async-start | bytes 5308416 | tf_op jit(solution)/shard_map/all_gather | solution.py:247
  42.7 39.1 %copy-start.89 = (s32[2,2048]{1,0:T(2,128)S(1)}, s32[2,2048]{1,0:T(2,128)}, u32[]{:S(2)}) copy-start(s32[2,2048]{1,0:T(2,128)} %param.19) | copy-start | bytes 49156
  42.7 439.5 %all-gather.22.cloned.1.call-start = ((), (), s32[]{:S(2)}) async-start(), calls=%async_computation.16 | async-start | bytes 5308416 | tf_op jit(solution)/shard_map/all_gather | solution.py:248
  43.4 38.4 %copy-start.120 = (bf16[384]{0:T(512)(128)(2,1)S(1)}, bf16[384]{0:T(512)(128)(2,1)}, u32[]{:S(2)}) copy-start(bf16[384]{0:T(512)(128)(2,1)} %param.30) | copy-start | bytes 2308
  43.4 847.3 %reduce-scatter.19.cloned.1.call-start = ((), (), s32[]{:S(2)}) async-start(), calls=%async_computation.19 | async-start | bytes 7864320 | tf_op jit(solution)/shard_map/reduce_scatter | solution.py:358
  76.6 23.4 %collective-permute-start = (bf16[512,768]{1,0:T(8,128)(2,1)S(1)}, bf16[512,768]{1,0:T(8,128)(2,1)}, u32[]{:S(2)}, u32[]{:S(2)}) collective-permute-start(bf16[512,768]{1,0:T(8,128)(2,1)S(1)} %add_convert_fusion.9), channel_id=1, source_target_pairs={{0,8},{8,16},{16,24},{24,0},{1,9},{9,17},{17,25},{25,1},{2,10},{10... | collective-permute-start | bytes 2359304 | tf_op jit(solution)/shard_map/ppermute | solution.py:21
  80.2 45.7 %collective-permute-start.3 = (bf16[512,768]{1,0:T(8,128)(2,1)S(1)}, bf16[512,768]{1,0:T(8,128)(2,1)}, u32[]{:S(2)}, u32[]{:S(2)}) collective-permute-start(bf16[512,768]{1,0:T(8,128)(2,1)S(1)} %add_convert_fusion.5), channel_id=1, source_target_pairs={{0,8},{8,16},{16,24},{24,0},{1,9},{9,17},{17,25},{25,1},{2,10},{10... | collective-permute-start | bytes 2359304 | tf_op jit(solution)/shard_map/ppermute | solution.py:21
  100.0 57.1 %collective-permute-start.1 = (bf16[512,768]{1,0:T(8,128)(2,1)}, bf16[512,768]{1,0:T(8,128)(2,1)}, u32[]{:S(2)}, u32[]{:S(2)}) collective-permute-start(bf16[512,768]{1,0:T(8,128)(2,1)} %collective-permute-done), channel_id=1, source_target_pairs={{0,8},{8,16},{16,24},{24,0},{1,9},{9,17},{17,25},{25,1},{2,10},{10... | collective-permute-start | bytes 2359304 | tf_op jit(solution)/shard_map/ppermute | solution.py:21
  125.9 54.9 %collective-permute-start.4 = (bf16[512,768]{1,0:T(8,128)(2,1)}, bf16[512,768]{1,0:T(8,128)(2,1)}, u32[]{:S(2)}, u32[]{:S(2)}) collective-permute-start(bf16[512,768]{1,0:T(8,128)(2,1)} %collective-permute-done.3), channel_id=1, source_target_pairs={{0,8},{8,16},{16,24},{24,0},{1,9},{9,17},{17,25},{25,1},{2,10},{10... | collective-permute-start | bytes 2359304 | tf_op jit(solution)/shard_map/ppermute | solution.py:21
  133.8 153.8 %copy-start = (bf16[512,768]{0,1:T(8,128)(2,1)}, bf16[512,768]{0,1:T(8,128)(2,1)S(1)}, u32[]{:S(2)}) copy-start(bf16[512,768]{0,1:T(8,128)(2,1)S(1)} %copy.198) | copy-start | bytes 2359300
  138.4 195.0 %copy-start.2 = (bf16[512,768]{0,1:T(8,128)(2,1)}, bf16[512,768]{0,1:T(8,128)(2,1)S(1)}, u32[]{:S(2)}) copy-start(bf16[512,768]{0,1:T(8,128)(2,1)S(1)} %copy.185) | copy-start | bytes 2359300
  138.4 50.8 %copy-start.61 = (bf16[512,768]{0,1:T(8,128)(2,1)S(1)}, bf16[512,768]{0,1:T(8,128)(2,1)}, u32[]{:S(2)}) copy-start(bf16[512,768]{0,1:T(8,128)(2,1)} %copy.181) | copy-start | bytes 2359300
  157.1 50.7 %collective-permute-start.2 = (bf16[512,768]{1,0:T(8,128)(2,1)}, bf16[512,768]{1,0:T(8,128)(2,1)}, u32[]{:S(2)}, u32[]{:S(2)}) collective-permute-start(bf16[512,768]{1,0:T(8,128)(2,1)} %collective-permute-done.1), channel_id=1, source_target_pairs={{0,8},{8,16},{16,24},{24,0},{1,9},{9,17},{17,25},{25,1},{2,10},{10... | collective-permute-start | bytes 2359304 | tf_op jit(solution)/shard_map/ppermute | solution.py:21
  180.8 47.5 %collective-permute-start.5 = (bf16[512,768]{1,0:T(8,128)(2,1)}, bf16[512,768]{1,0:T(8,128)(2,1)}, u32[]{:S(2)}, u32[]{:S(2)}) collective-permute-start(bf16[512,768]{1,0:T(8,128)(2,1)} %collective-permute-done.4), channel_id=1, source_target_pairs={{0,8},{8,16},{16,24},{24,0},{1,9},{9,17},{17,25},{25,1},{2,10},{10... | collective-permute-start | bytes 2359304 | tf_op jit(solution)/shard_map/ppermute | solution.py:21
  312.4 104.4 %copy-start.83 = (f32[12,512]{1,0:T(8,128)}, f32[12,512]{1,0:T(8,128)S(1)}, u32[]{:S(2)}) copy-start(f32[12,512]{1,0:T(8,128)S(1)} %log_add_fusion) | copy-start | bytes 73732
  357.4 39.3 %copy-start.85 = (f32[12,512]{1,0:T(8,128)}, f32[12,512]{1,0:T(8,128)S(1)}, u32[]{:S(2)}) copy-start(f32[12,512]{1,0:T(8,128)S(1)} %log_add_fusion.1) | copy-start | bytes 73732
  357.4 39.3 %copy-start.45 = (bf16[512,768]{0,1:T(8,128)(2,1)S(1)}, bf16[512,768]{0,1:T(8,128)(2,1)}, u32[]{:S(2)}) copy-start(bf16[512,768]{0,1:T(8,128)(2,1)} %get-tuple-element.139) | copy-start | bytes 2359300
  412.9 43.1 %copy-start.62 = (bf16[12,64,512]{2,1,0:T(8,128)(2,1)}, bf16[12,64,512]{2,1,0:T(8,128)(2,1)S(1)}, u32[]{:S(2)}) copy-start(bf16[12,64,512]{2,1,0:T(8,128)(2,1)S(1)} %add_convert_fusion.7) | copy-start | bytes 2359300
  415.4 118.2 %copy-start.95 = (f32[512]{0:T(512)}, f32[512]{0:T(512)S(1)}, u32[]{:S(2)}) copy-start(f32[512]{0:T(512)S(1)} %broadcast_multiply_fusion.3) | copy-start | bytes 6148
  416.9 39.2 %copy-start.37 = (bf16[512,768]{0,1:T(8,128)(2,1)S(1)}, bf16[512,768]{0,1:T(8,128)(2,1)}, u32[]{:S(2)}) copy-start(bf16[512,768]{0,1:T(8,128)(2,1)} %get-tuple-element.147) | copy-start | bytes 2359300
  473.3 60.3 %copy-start.6 = (f32[512,768]{1,0:T(8,128)}, f32[512,768]{1,0:T(8,128)S(1)}, u32[]{:S(2)}) copy-start(f32[512,768]{1,0:T(8,128)S(1)} %get-tuple-element.207) | copy-start | bytes 4718596
  473.4 60.3 %copy-start.90 = (f32[512]{0:T(512)}, f32[512]{0:T(512)S(1)}, u32[]{:S(2)}) copy-start(f32[512]{0:T(512)S(1)} %broadcast_multiply_fusion.1) | copy-start | bytes 6148
  473.7 60.0 %copy-start.112 = (f32[512]{0:T(512)}, f32[512]{0:T(512)S(1)}, u32[]{:S(2)}) copy-start(f32[512]{0:T(512)S(1)} %fusion.175) | copy-start | bytes 6148
  473.7 60.0 %copy-start.93 = (f32[512]{0:T(512)}, f32[512]{0:T(512)S(1)}, u32[]{:S(2)}) copy-start(f32[512]{0:T(512)S(1)} %fusion.177) | copy-start | bytes 6148
  560.3 334.1 %reduce-scatter.23.cloned.1.call-start = ((), (), s32[]{:S(2)}) async-start(), calls=%async_computation.21 | async-start | bytes 7864320 | tf_op jit(solution)/shard_map/reduce_scatter | solution.py:358
  614.1 77.4 %copy-start.3 = (bf16[512,768]{0,1:T(8,128)(2,1)S(1)}, bf16[512,768]{0,1:T(8,128)(2,1)}, u32[]{:S(2)}) copy-start(bf16[512,768]{0,1:T(8,128)(2,1)} %copy-done.2) | copy-start | bytes 2359300
  614.1 287.8 %reduce-scatter.17.cloned.1.call-start = ((), (), s32[]{:S(2)}) async-start(), calls=%async_computation.18 | async-start | bytes 7864320 | tf_op jit(solution)/shard_map/reduce_scatter | solution.py:352
  739.5 87.7 %copy-start.1 = (bf16[512,768]{0,1:T(8,128)(2,1)S(1)}, bf16[512,768]{0,1:T(8,128)(2,1)}, u32[]{:S(2)}) copy-start(bf16[512,768]{0,1:T(8,128)(2,1)} %copy-done) | copy-start | bytes 2359300
  739.5 178.5 %reduce-scatter.21.cloned.1.call-start = ((), (), s32[]{:S(2)}) async-start(), calls=%async_computation.20 | async-start | bytes 7864320 | tf_op jit(solution)/shard_map/reduce_scatter | solution.py:352
  849.4 115.4 %reduce-scatter.25.cloned.1.call-start = ((), (), s32[]{:S(2)}) async-start(), calls=%async_computation.22 | async-start | bytes 2654208 | tf_op jit(solution)/shard_map/reduce_scatter | solution.py:393
  853.8 140.4 %reduce-scatter.31.cloned.1.call-start = ((), (), s32[]{:S(2)}) async-start(), calls=%async_computation.25 | async-start | bytes 2654208
  890.7 141.2 %reduce-scatter.35.cloned.1.call-start = ((), (), s32[]{:S(2)}) async-start(), calls=%async_computation.27 | async-start | bytes 2654208
  901.9 167.8 %reduce-scatter.33.cloned.1.call-start = ((), (), s32[]{:S(2)}) async-start(), calls=%async_computation.26 | async-start | bytes 2654208
  925.5 245.0 %reduce-scatter.29.cloned.1.call-start = ((), (), s32[]{:S(2)}) async-start(), calls=%async_computation.24 | async-start | bytes 10616832 | tf_op jit(solution)/shard_map/reduce_scatter | solution.py:393
  942.1 328.4 %reduce-scatter.27.cloned.1.call-start = ((), (), s32[]{:S(2)}) async-start(), calls=%async_computation.23 | async-start | bytes 10616832 | tf_op jit(solution)/shard_map/reduce_scatter | solution.py:393
  954.4 387.4 %all-reduce.23.cloned.1.call-start = ((), (), s32[]{:S(2)}) async-start(), calls=%async_computation.28 | async-start | bytes 3833856 | tf_op jit(solution)/shard_map/psum | solution.py:394
  958.1 37.9 %copy-start.11 = (f32[512,768]{0,1:T(8,128)S(1)}, f32[512,768]{0,1:T(8,128)}, u32[]{:S(2)}) copy-start(f32[512,768]{0,1:T(8,128)} %reduce-scatter.19.cloned.1.call-done) | copy-start | bytes 4718596
  964.9 307.9 %copy-start.8 = (f32[512,768]{0,1:T(8,128)S(1)}, f32[512,768]{0,1:T(8,128)}, u32[]{:S(2)}) copy-start(f32[512,768]{0,1:T(8,128)} %reduce-scatter.23.cloned.1.call-done) | copy-start | bytes 4718596
  1272.9 46.6 %copy-start.98 = (f32[512]{0:T(512)S(1)}, f32[512]{0:T(512)}, u32[]{:S(2)}) copy-start(f32[512]{0:T(512)} %copy-done.97) | copy-start | bytes 6148
  (120 other events, 815.2 us)
Sparse Core Ops, SparseCore 0:
  9.7 25.3 all-gather.13
  36.7 22.5 all-gather.9
  61.0 22.3 all-gather.11
  85.0 69.7 all-gather.23
  156.6 68.2 all-gather.15
  226.3 22.6 all-gather.17
  250.7 51.4 all-gather.19
  303.8 50.5 all-gather.21
  560.5 68.4 reduce-scatter.18
  631.8 70.1 reduce-scatter.22
  739.6 67.8 reduce-scatter.16
  849.6 68.3 reduce-scatter.20
  920.3 36.1 reduce-scatter.24
  958.7 35.4 reduce-scatter.30
  996.4 35.4 reduce-scatter.34
  1034.1 35.5 reduce-scatter.32
  1071.8 98.6 reduce-scatter.28
  1172.6 97.8 reduce-scatter.26
  1275.0 66.8 all-reduce.22
